TPU v7x, 128 devices: a whole 4x4x4 slice. The times are simulated.
128 devices in a mesh: prow: 8 (over z, core), pcol: 16 (over x, y).
Axes of the slice: x: 4, y: 4, z: 4, core: 2. Of those that a mesh axis runs over, the one named last changes fastest.
Arguments:
- factors: bfloat16 [4, 4096, 512], P(None, ('prow', 'pcol')), may hold values from -0.25 to 0.25
- x_factor: bfloat16 [512, 512], replicated, may hold values from -0.25 to 0.25
- zinv_factor: bfloat16 [512, 512], replicated, may hold values from -0.25 to 0.25
- placement: int32 [4096], replicated, may hold values from 0 to 4095, as said below
Outputs:
- trailing: float32 [4096, 4096], P('prow', 'pcol')
- panels: float32 [4096, 1024], P('prow', 'pcol')
Inputs may be any that keep to these rules, and one draw needn't show every extreme that they name: placement is a permutation of the Schur rows; device d (grid rows slowest) assembles the rows placement[d * 32] to placement[d * 32 + 31]; among one device's rows at most 8 share the same owner grid row (natural row i belongs to grid row (i div 64) mod 8), and some device has exactly 8 such rows.
All inputs are finite; a program needn't handle non-finite values.
Results may differ from a plain program's by a relative error of at most 0.003.
Values may be sent and summed in bfloat16 or wider, within the bound.
A program may use at most 128 MiB of HBM per device.

v0:
```python
import jax
import jax.numpy as jnp
from jax import lax
from jax.sharding import PartitionSpec as P

RANK = 4
NB = 64
K = 1024
rank_signs = (1.0, 1.0, -1.0, -1.0)


def project(segment, factor_mat):
    span_cols = segment.shape[1]
    flat_rows = segment.reshape(RANK * span_cols, segment.shape[2])
    images = jnp.dot(flat_rows, factor_mat, preferred_element_type=jnp.float32).astype(jnp.bfloat16)
    return images.reshape(RANK, span_cols, factor_mat.shape[1])


def pair_terms(left_x, left_z, right_x, right_z):
    weights = jnp.array(rank_signs, jnp.float32)
    contract = (((1,), (1,)), ((), ()))
    span_rows = left_x.shape[1]
    span_cols = right_x.shape[1]
    width = left_x.shape[2]
    inner_x = lax.dot_general(
        left_x.reshape(RANK * span_rows, width),
        right_x.reshape(RANK * span_cols, width),
        contract,
        preferred_element_type=jnp.float32,
    )
    inner_z = lax.dot_general(
        left_z.reshape(RANK * span_rows, width),
        right_z.reshape(RANK * span_cols, width),
        contract,
        preferred_element_type=jnp.float32,
    )
    product = (inner_x * inner_z).reshape(RANK, span_rows, RANK, span_cols)
    return jnp.einsum("r,riqj,q->ij", weights, product, weights)


def per_device(factors, x_factor, zinv_factor, placement):
    prow_count = lax.axis_size("prow")
    pcol_count = lax.axis_size("pcol")
    devices_all = prow_count * pcol_count
    rows_dev = factors.shape[1]
    total_rows = placement.shape[0]
    local_rows = total_rows // prow_count
    local_cols = total_rows // pcol_count
    prow_id = lax.axis_index("prow")
    pcol_id = lax.axis_index("pcol")
    inverse = (
        jnp.zeros((total_rows,), jnp.int32)
        .at[placement]
        .set(jnp.arange(total_rows, dtype=jnp.int32))
    )
    slot_k = jnp.arange(local_rows)
    natural_k = slot_k // NB * NB * prow_count + prow_id * NB + slot_k % NB
    own_x = project(factors, x_factor)
    own_z = project(factors, zinv_factor)
    blank_rows = jnp.zeros((rows_dev, total_rows), jnp.float32)
    schur_rows = blank_rows.at[:, placement].set(
        pair_terms(
            own_x,
            own_z,
            lax.all_gather(own_x, ("prow", "pcol"), axis=1, tiled=True),
            lax.all_gather(own_z, ("prow", "pcol"), axis=1, tiled=True),
        )
    )
    device_id = lax.axis_index(("prow", "pcol"))
    my_rows = lax.dynamic_slice_in_dim(placement, device_id * rows_dev, rows_dev)
    capacity = 2 * rows_dev // prow_count
    target = my_rows // NB % prow_count
    prow_ids = jnp.arange(prow_count)
    onehot = (target[:, None] == prow_ids[None, :]).astype(jnp.int32)
    rank_in = jnp.sum((jnp.cumsum(onehot, axis=0) - onehot) * onehot, axis=1)
    select = (
        (target[None, None, :] == prow_ids[:, None, None])
        & (rank_in[None, None, :] == jnp.arange(capacity)[None, :, None])
    ).astype(jnp.float32)
    packed = jnp.dot(
        select.reshape(prow_count * capacity, rows_dev), schur_rows, precision=lax.Precision.HIGHEST
    )
    packed = packed.reshape(prow_count, capacity, total_rows // (NB * pcol_count), pcol_count, NB)
    packed = packed.transpose(0, 3, 1, 2, 4).reshape(prow_count, pcol_count, capacity, local_cols)
    received = lax.all_to_all(
        packed.reshape(devices_all, capacity, local_cols),
        ("prow", "pcol"),
        split_axis=0,
        concat_axis=0,
        tiled=True,
    )
    received = received.reshape(devices_all * capacity, local_cols)
    all_target = (placement // NB % prow_count).reshape(devices_all, rows_dev)
    earlier = jnp.arange(rows_dev)[None, :, None] > jnp.arange(rows_dev)[None, None, :]
    slot_ranks = jnp.sum(
        ((all_target[:, :, None] == all_target[:, None, :]) & earlier).astype(jnp.int32), axis=2
    ).reshape(total_rows)
    position = inverse[natural_k]
    flat_index = position // rows_dev * capacity + slot_ranks[position]
    schur_local = received[flat_index]
    lead_cols = K // pcol_count
    front_cols = schur_local[:, :lead_cols]
    row_panel = lax.all_gather(front_cols, "pcol", axis=1, tiled=True)
    row_panel = (
        row_panel.reshape(local_rows, pcol_count, lead_cols // NB, NB)
        .transpose(0, 2, 1, 3)
        .reshape(local_rows, K)
    )
    lead_rows = K // prow_count
    top_panel, top_cols = (
        lax.all_gather(row_panel[:lead_rows], "prow", axis=0, tiled=True),
        lax.all_gather(schur_local[:lead_rows], "prow", axis=0, tiled=True),
    )

    def natural_rows(stacked):
        return (
            stacked.reshape(prow_count, lead_rows // NB, NB, stacked.shape[1])
            .transpose(1, 0, 2, 3)
            .reshape(K, stacked.shape[1])
        )

    leading = jnp.linalg.cholesky(natural_rows(top_panel))
    panel_rows = lax.linalg.triangular_solve(
        leading, row_panel, left_side=False, lower=True, transpose_a=True
    )
    panel_cols = lax.linalg.triangular_solve(
        leading, natural_rows(top_cols).T, left_side=False, lower=True, transpose_a=True
    )
    trailing = schur_local - jnp.dot(panel_rows, panel_cols.T, precision=lax.Precision.HIGHEST)
    own_panel = lax.dynamic_index_in_dim(
        panel_rows.reshape(local_rows, K // (NB * pcol_count), pcol_count, NB),
        pcol_id,
        2,
        keepdims=False,
    )
    return (trailing, own_panel.reshape(local_rows, K // pcol_count))


def solution(mesh):
    in_specs = (P(None, ("prow", "pcol"), None), P(), P(), P())
    out_specs = (P("prow", "pcol"), P("prow", "pcol"))
    return jax.shard_map(
        per_device, mesh=mesh, in_specs=in_specs, out_specs=out_specs, check_vma=False
    )
```

profile of v0, /device:TPU:1, one launch (start us, length us, event | category | flops | bytes accessed | tf_op | source)
XLA Modules:
  0.0 744.0 jit_solution(3466437488755991065)
XLA Ops:
  14.9 80.7 %all-gather.6.cloned.1.call-done = bf16[4,4096,512]{2,1,0:T(8,128)(2,1)} async-done(((bf16[4,32,512]{2,1,0:T(8,128)(2,1)}), bf16[4,4096,512]{2,1,0:T(8,128)(2,1)}) %all-gather.6.cloned.1.call-update) | async-done | bytes 16777232 | tf_op jit(solution)/shard_map/all_gather | solution.py:65
  95.5 14.6 %fusion.113 = f32[128,16384]{1,0:T(8,128)} fusion(bf16[128,512]{1,0:T(8,128)(2,1)} %convolution_convert_fusion.1, bf16[16384,512]{1,0:T(8,128)(2,1)} %bitcast.189), kind=kOutput, calls=%fused_computation.289 | convolution fusion | flops 2147483648 | bytes 25296896 | tf_op jit(solution)/shard_map/dot_general | solution.py:25
  110.1 68.9 %all-gather.8.cloned.1.call-done = bf16[4,4096,512]{2,1,0:T(8,128)(2,1)} async-done(((bf16[4,32,512]{2,1,0:T(8,128)(2,1)}), bf16[4,4096,512]{2,1,0:T(8,128)(2,1)}) %all-gather.8.cloned.1.call-update) | async-done | bytes 16777232 | tf_op jit(solution)/shard_map/all_gather | solution.py:66
  179.0 12.9 %convolution_multiply_fusion = f32[128,16384]{1,0:T(8,128)} fusion(f32[128,16384]{1,0:T(8,128)} %fusion.113, bf16[128,512]{1,0:T(8,128)(2,1)S(1)} %copy-done.4, bf16[16384,512]{1,0:T(8,128)(2,1)} %bitcast.187), kind=kOutput, calls=%fused_computation.7 | convolution fusion | flops 2149580800 | bytes 33685504 | tf_op jit(solution)/shard_map/dot_general | solution.py:31
  191.9 10.8 %reshape.351 = f32[4,32,4,4096]{3,2,1,0:T(4,128)} reshape(f32[128,16384]{1,0:T(8,128)} %convolution_multiply_fusion) | data formatting | bytes 16777216 | tf_op jit(solution)/shard_map/reshape | solution.py:37
  202.7 6.4 multiply_reduce_fusion
  209.8 12.5 %scatter_custom_fusion = f32[32,4096]{0,1:T(8,128)} fusion(s32[4096]{0:T(1024)S(1)} %get-tuple-element.100, f32[32,4096]{0,1:T(8,128)S(1)} %copy.66, f32[]{:T(128)} %constant.382.clone.1), kind=kCustom, calls=%fused_computation.13 | custom fusion | bytes 2621444 | tf_op jit(solution)/shard_map/scatter | solution.py:61
  230.5 7.4 all-to-all-start
  238.0 15.5 %scatter_custom_fusion.1 = s32[4096]{0:T(1024)S(1)} fusion(s32[4096]{0:T(1024)S(1)} %get-tuple-element.100, s32[4096]{0:T(1024)S(1)} %iota.176, s32[]{:T(128)} %copy.145), kind=kCustom, calls=%fused_computation.235 | custom fusion | bytes 16388 | tf_op jit(solution)/shard_map/scatter | solution.py:54
  263.7 44.1 %all-gather.10.cloned.1.call-done = f32[512,1024]{0,1:T(8,128)} async-done(((f32[512,64]{0,1:T(8,128)}), f32[512,1024]{0,1:T(8,128)}) %all-gather.10.cloned.1.call-update) | async-done | bytes 2097168 | tf_op jit(solution)/shard_map/all_gather | solution.py:103
  309.9 24.3 %all-gather.14.cloned.1.call-done = f32[1024,256]{1,0:T(8,128)} async-done(((f32[128,256]{1,0:T(8,128)}), f32[1024,256]{1,0:T(8,128)}) %all-gather.14.cloned.1.call-update) | async-done | bytes 1048592 | tf_op jit(solution)/shard_map/all_gather | solution.py:112
  341.1 27.4 %all-gather.12.cloned.1.call-done = f32[1024,1024]{1,0:T(8,128)} async-done(((f32[128,1024]{1,0:T(8,128)}), f32[1024,1024]{1,0:T(8,128)}) %all-gather.12.cloned.1.call-update) | async-done | bytes 4194320 | tf_op jit(solution)/shard_map/all_gather | solution.py:111
  368.5 4.7 copy.50
  373.2 5.5 copy.51
  385.1 11.7 %cholesky.223 = f32[128,128]{1,0:T(8,128)S(1)} custom-call(f32[128,128]{1,0:T(8,128)S(1)} %cholesky.580), custom_call_target="Cholesky" | custom-call | tf_op jit(solution)/shard_map/jit(cholesky)/cholesky | solution.py:122
  399.4 9.8 %custom-call.64 = f32[1,128,128]{1,2,0:T(8,128)S(1)} custom-call(f32[1,128,128]{2,1,0:T(8,128)S(1)} %get-tuple-element.98), custom_call_target="InvertDiagBlocksLowerTriangular" | custom-call | tf_op jit(solution)/shard_map/jit(cholesky)/cholesky | solution.py:122
  413.1 11.9 %cholesky.244 = f32[128,128]{1,0:T(8,128)S(1)} custom-call(f32[128,128]{1,0:T(8,128)S(1)} %cholesky.584), custom_call_target="Cholesky" | custom-call | tf_op jit(solution)/shard_map/jit(cholesky)/cholesky | solution.py:122
  426.9 9.8 %custom-call.65 = f32[1,128,128]{1,2,0:T(8,128)S(1)} custom-call(f32[1,128,128]{2,1,0:T(8,128)S(1)} %get-tuple-element.95), custom_call_target="InvertDiagBlocksLowerTriangular" | custom-call | tf_op jit(solution)/shard_map/jit(cholesky)/cholesky | solution.py:122
  440.1 11.7 %cholesky.468 = f32[128,128]{1,0:T(8,128)S(1)} custom-call(f32[128,128]{1,0:T(8,128)S(1)} %cholesky.589), custom_call_target="Cholesky" | custom-call | tf_op jit(solution)/shard_map/jit(cholesky)/cholesky | solution.py:122
  453.2 9.8 %custom-call.66 = f32[1,128,128]{1,2,0:T(8,128)S(1)} custom-call(f32[1,128,128]{2,1,0:T(8,128)S(1)} %get-tuple-element.92), custom_call_target="InvertDiagBlocksLowerTriangular" | custom-call | tf_op jit(solution)/shard_map/jit(cholesky)/cholesky | solution.py:122
  466.5 12.1 %cholesky.487 = f32[128,128]{1,0:T(8,128)S(1)} custom-call(f32[128,128]{1,0:T(8,128)S(1)} %cholesky.594), custom_call_target="Cholesky" | custom-call | tf_op jit(solution)/shard_map/jit(cholesky)/cholesky | solution.py:122
  479.9 9.8 %custom-call.67 = f32[1,128,128]{1,2,0:T(8,128)S(1)} custom-call(f32[1,128,128]{2,1,0:T(8,128)S(1)} %get-tuple-element.89), custom_call_target="InvertDiagBlocksLowerTriangular" | custom-call | tf_op jit(solution)/shard_map/jit(cholesky)/cholesky | solution.py:122
  493.2 11.7 %cholesky.506 = f32[128,128]{1,0:T(8,128)S(1)} custom-call(f32[128,128]{1,0:T(8,128)S(1)} %cholesky.599), custom_call_target="Cholesky" | custom-call | tf_op jit(solution)/shard_map/jit(cholesky)/cholesky | solution.py:122
  506.3 9.9 %custom-call.68 = f32[1,128,128]{1,2,0:T(8,128)S(1)} custom-call(f32[1,128,128]{2,1,0:T(8,128)S(1)} %get-tuple-element.86), custom_call_target="InvertDiagBlocksLowerTriangular" | custom-call | tf_op jit(solution)/shard_map/jit(cholesky)/cholesky | solution.py:122
  519.6 11.7 %cholesky.526 = f32[128,128]{1,0:T(8,128)S(1)} custom-call(f32[128,128]{1,0:T(8,128)S(1)} %cholesky.604), custom_call_target="Cholesky" | custom-call | tf_op jit(solution)/shard_map/jit(cholesky)/cholesky | solution.py:122
  532.6 9.8 %custom-call.69 = f32[1,128,128]{1,2,0:T(8,128)S(1)} custom-call(f32[1,128,128]{2,1,0:T(8,128)S(1)} %get-tuple-element.83), custom_call_target="InvertDiagBlocksLowerTriangular" | custom-call | tf_op jit(solution)/shard_map/jit(cholesky)/cholesky | solution.py:122
  545.4 11.9 %cholesky.546 = f32[128,128]{1,0:T(8,128)S(1)} custom-call(f32[128,128]{1,0:T(8,128)S(1)} %cholesky.609), custom_call_target="Cholesky" | custom-call | tf_op jit(solution)/shard_map/jit(cholesky)/cholesky | solution.py:122
  558.5 9.8 %custom-call.70 = f32[1,128,128]{1,2,0:T(8,128)S(1)} custom-call(f32[1,128,128]{2,1,0:T(8,128)S(1)} %get-tuple-element.80), custom_call_target="InvertDiagBlocksLowerTriangular" | custom-call | tf_op jit(solution)/shard_map/jit(cholesky)/cholesky | solution.py:122
  571.0 11.7 %cholesky.564 = f32[128,128]{1,0:T(8,128)S(1)} custom-call(f32[128,128]{1,0:T(8,128)S(1)} %convolution_subtract_fusion.21), custom_call_target="Cholesky" | custom-call | tf_op jit(solution)/shard_map/jit(cholesky)/cholesky | solution.py:122
  589.2 4.8 select_select_fusion
  594.0 28.0 %while.1 = (s32[]{:T(128)}, f32[1024,1024]{1,0:T(8,128)}, s32[8,2]{0,1:T(2,128)S(1)}, f32[8,128,128]{2,1,0:T(8,128)}, s32[]{:T(128)}) while((s32[]{:T(128)}, f32[1024,1024]{1,0:T(8,128)}, s32[8,2]{0,1:T(2,128)S(1)}, f32[8,128,128]{2,1,0:T(8,128)}, s32[]{:T(128)}) %tuple.90), condition=%wide.while_cond, body=%wide.while_body.sunk | while | flops 2 | bytes 132705 | solution.py:123
  622.0 79.8 %custom-call.71 = f32[8,128,128]{1,2,0:T(8,128)S(1)} custom-call(f32[8,128,128]{2,1,0:T(8,128)} %get-tuple-element.9), custom_call_target="InvertDiagBlocksLowerTriangular" | custom-call | tf_op jit(solution)/shard_map/triangular_solve | solution.py:123
  (172 shorter events, 140.7 us)
Async XLA Ops:
  7.2 1.1 copy-start
  7.2 88.4 %all-gather.6.cloned.1.call-start = ((), (), s32[]{:S(2)}) async-start(), calls=%async_computation.1 | async-start | bytes 16908288 | tf_op jit(solution)/shard_map/all_gather | solution.py:65
  10.0 168.9 %all-gather.8.cloned.1.call-start = ((), (), s32[]{:S(2)}) async-start(), calls=%async_computation.2 | async-start | bytes 16908288 | tf_op jit(solution)/shard_map/all_gather | solution.py:66
  95.5 83.4 %copy-start.4 = (bf16[128,512]{1,0:T(8,128)(2,1)S(1)}, bf16[128,512]{1,0:T(8,128)(2,1)}, u32[]{:S(2)}) copy-start(bf16[128,512]{1,0:T(8,128)(2,1)} %convolution_convert_fusion) | copy-start | bytes 393220
  230.5 30.0 %all-to-all-start = ((f32[128,8,256]{2,1,0:T(8,128)}), f32[128,8,256]{2,1,0:T(8,128)S(1)}, u32[]{:S(2)}, u32[]{:S(2)}) async-start(f32[128,8,256]{2,1,0:T(8,128)} %reshape_reshape.3), calls=%async_computation | async-start | bytes 2097152 | tf_op jit(solution)/shard_map/all_to_all | solution.py:85
  237.9 69.8 %all-gather.10.cloned.1.call-start = ((), (), s32[]{:S(2)}) async-start(), calls=%async_computation.3 | async-start | bytes 2228224 | tf_op jit(solution)/shard_map/all_gather | solution.py:103
  262.9 71.2 %all-gather.14.cloned.1.call-start = ((), (), s32[]{:S(2)}) async-start(), calls=%async_computation.5 | async-start | bytes 1179648 | tf_op jit(solution)/shard_map/all_gather | solution.py:112
  263.6 104.9 %all-gather.12.cloned.1.call-start = ((), (), s32[]{:S(2)}) async-start(), calls=%async_computation.4 | async-start | bytes 4718592 | tf_op jit(solution)/shard_map/all_gather | solution.py:111
  383.2 1.9 copy-start.3
  701.8 6.0 copy-start.2
  708.8 7.1 copy-start.5
  710.4 6.6 copy-start.6
  716.0 4.7 copy-start.8
  722.5 6.2 copy-start.7
  728.2 9.0 %copy-start.1 = (bf16[512,512]{1,0:T(8,128)(2,1)S(1)}, bf16[512,512]{1,0:T(8,128)(2,1)}, u32[]{:S(2)}) copy-start(bf16[512,512]{1,0:T(8,128)(2,1)} %param.6) | copy-start | bytes 1572868
Sparse Core Ops, SparseCore 0:
  11.6 83.9 all-gather.5
  99.1 79.8 all-gather.7
  263.0 44.6 all-gather.9
  309.3 24.7 all-gather.13
  336.3 32.1 all-gather.11
where the time goes:
time: 754 us; the launch traced here: 744 us
  other arithmetic  272 us (36%)
  waiting for transfers between devices  245 us (32%)
  local copies, waits for them, and re-layouts  106 us (14%)
  matrix products  93.6 us (12%)
  between operations  19.9 us (3%)
  starting transfers between devices  7.58 us (1%)
    another operation x31, other arithmetic, per_device(): leading = jnp.linalg.cholesky(natural_rows(top_panel))  173 us
    another operation x3, other arithmetic, per_device(): lax.linalg.triangular_solve(leading, row_panel, left_side=False, lower=Tr...  84.6 us
    all_gather x1, waiting for transfers between devices, per_device(): lax.all_gather(own_x, ('prow', 'pcol'), axis=1, tiled=True)  80.7 us
    all_gather x1, waiting for transfers between devices, per_device(): lax.all_gather(own_z, ('prow', 'pcol'), axis=1, tiled=True)  68.9 us
    all_gather x1, waiting for transfers between devices, per_device(): row_panel = lax.all_gather(front_cols, 'pcol', axis=1, tiled=True)  44.1 us
    another operation x24, local copies, waits for them, and re-layouts  28 us
    all_gather x1, waiting for transfers between devices, per_device(): lax.all_gather(row_panel[:lead_rows], 'prow', axis=0, tiled=True)  27.4 us
    all_gather x1, waiting for transfers between devices, per_device(): lax.all_gather(schur_local[:lead_rows], 'prow', axis=0, tiled=True)  24.3 us
  transfers between devices with their start and end apart: 6, of which 5 were waited for; matrix products, arithmetic and copies ran while one was open for 7% of the time, Pallas kernels for 0%

commit v1 on v0

--- a/solution.py
+++ b/solution.py
@@ -63,7 +63,12 @@
             own_x,
             own_z,
             lax.all_gather(own_x, ("prow", "pcol"), axis=1, tiled=True),
-            lax.all_gather(own_z, ("prow", "pcol"), axis=1, tiled=True),
+            jnp.concatenate(
+                lax.all_to_all(
+                    jnp.stack([own_z] * lax.axis_size(("prow", "pcol"))), ("prow", "pcol"), 0, 0
+                ),
+                axis=1,
+            ),
         )
     )
     device_id = lax.axis_index(("prow", "pcol"))

time: 754 us -> 895 us (1.19)
  waiting for transfers between devices: 245 us -> 356 us
  local copies, waits for them, and re-layouts: 106 us -> 126 us
  starting transfers between devices: 7.58 us -> 20.6 us
    all_to_all x0 -> x1, waiting for transfers between devices: none -> 260 us  [per_device(): lax.all_to_all(jnp.stack([own_z] * lax.axis_size(('prow', 'pcol'))), ('pr...]
    all_gather x1, waiting for transfers between devices: 80.7 us -> 0.01 us  [per_device(): lax.all_gather(own_x, ('prow', 'pcol'), axis=1, tiled=True)]
    all_gather x1 -> x0, waiting for transfers between devices: 68.9 us -> none  [per_device(): lax.all_gather(own_z, ('prow', 'pcol'), axis=1, tiled=True)]
    all_to_all x0 -> x1, local copies, waits for them, and re-layouts: none -> 14.1 us  [per_device(): lax.all_to_all(jnp.stack([own_z] * lax.axis_size(('prow', 'pcol'))), ('pr...]
    all_to_all x0 -> x1, starting transfers between devices: none -> 11.9 us  [per_device(): lax.all_to_all(jnp.stack([own_z] * lax.axis_size(('prow', 'pcol'))), ('pr...]
    another operation x24 -> x25, local copies, waits for them, and re-layouts: 28 us -> 34 us
  transfers between devices with their start and end apart: 6 -> 6, of which waited for: 5 -> 4; matrix products, arithmetic and copies ran while one was open for 7% -> 6% of each run, Pallas kernels for 0% -> 0%
where the time goes in v1:
time: 895 us; the launch traced here: 885 us
  waiting for transfers between devices  356 us (40%)
  other arithmetic  269 us (30%)
  local copies, waits for them, and re-layouts  126 us (14%)
  matrix products  92.8 us (10%)
  starting transfers between devices  20.6 us (2%)
  between operations  19.9 us (2%)
    all_to_all x1, waiting for transfers between devices, per_device(): lax.all_to_all(jnp.stack([own_z] * lax.axis_size(('prow', 'pcol'))), ('pr...  260 us
    another operation x31, other arithmetic, per_device(): leading = jnp.linalg.cholesky(natural_rows(top_panel))  173 us
    another operation x3, other arithmetic, per_device(): lax.linalg.triangular_solve(leading, row_panel, left_side=False, lower=Tr...  84.6 us
    all_gather x1, waiting for transfers between devices, per_device(): row_panel = lax.all_gather(front_cols, 'pcol', axis=1, tiled=True)  44 us
    another operation x24, local copies, waits for them, and re-layouts  28 us
    all_gather x1, waiting for transfers between devices, per_device(): lax.all_gather(row_panel[:lead_rows], 'prow', axis=0, tiled=True)  27.4 us
    all_gather x1, waiting for transfers between devices, per_device(): lax.all_gather(schur_local[:lead_rows], 'prow', axis=0, tiled=True)  24.4 us
    another operation x14, matrix products, per_device(): leading = jnp.linalg.cholesky(natural_rows(top_panel))  23.1 us
  transfers between devices with their start and end apart: 6, of which 4 were waited for; matrix products, arithmetic and copies ran while one was open for 6% of the time, Pallas kernels for 0%

profile of v1, /device:TPU:1, one launch (start us, length us, event | category | flops | bytes accessed | tf_op | source)
XLA Modules:
  0.0 884.6 jit_solution(13920689809044193173)
XLA Ops:
  11.4 6.0 stack.3
  17.4 11.9 %all-to-all-start = ((bf16[128,4,32,512]{3,2,1,0:T(8,128)(2,1)}), bf16[128,4,32,512]{3,2,1,0:T(8,128)(2,1)}, u32[]{:S(2)}, u32[]{:S(2)}) async-start(bf16[128,4,32,512]{3,2,1,0:T(8,128)(2,1)} %stack.3), calls=%async_computation | async-start | bytes 33554432 | tf_op jit(solution)/shard_map/all_to_all | solution.py:67
  30.0 259.7 %all-to-all-done = bf16[128,4,32,512]{3,2,1,0:T(8,128)(2,1)} async-done(((bf16[128,4,32,512]{3,2,1,0:T(8,128)(2,1)}), bf16[128,4,32,512]{3,2,1,0:T(8,128)(2,1)}, u32[]{:S(2)}, u32[]{:S(2)}) %all-to-all-start) | async-done | bytes 16777248 | tf_op jit(solution)/shard_map/all_to_all | solution.py:67
  289.7 14.1 %copy.45 = bf16[128,4,32,512]{3,2,0,1:T(8,128)(2,1)} copy(bf16[128,4,32,512]{3,2,1,0:T(8,128)(2,1)} %all-to-all-done) | data formatting | bytes 33554432 | tf_op jit(solution)/shard_map/all_to_all | solution.py:67
  303.8 14.5 %fusion.113 = f32[128,16384]{1,0:T(8,128)} fusion(bf16[128,512]{1,0:T(8,128)(2,1)S(1)} %copy-done.4, bf16[16384,512]{1,0:T(8,128)(2,1)} %bitcast.191), kind=kOutput, calls=%fused_computation.289 | convolution fusion | flops 2147483648 | bytes 25296896 | tf_op jit(solution)/shard_map/dot_general | solution.py:25
  318.3 12.9 %convolution_multiply_fusion = f32[128,16384]{1,0:T(8,128)} fusion(f32[128,16384]{1,0:T(8,128)} %fusion.113, bf16[128,512]{1,0:T(8,128)(2,1)S(1)} %convolution_convert_fusion, bf16[16384,512]{1,0:T(8,128)(2,1)} %bitcast.188), kind=kOutput, calls=%fused_computation.7 | convolution fusion | flops 2149580800 | bytes 33685504 | tf_op jit(solution)/shard_map/dot_general | solution.py:31
  331.2 10.8 %reshape.349 = f32[4,32,4,4096]{3,2,1,0:T(4,128)} reshape(f32[128,16384]{1,0:T(8,128)} %convolution_multiply_fusion) | data formatting | bytes 16777216 | tf_op jit(solution)/shard_map/reshape | solution.py:37
  342.0 6.4 multiply_reduce_fusion
  349.1 12.5 %scatter_custom_fusion = f32[32,4096]{0,1:T(8,128)} fusion(s32[4096]{0:T(1024)S(1)} %get-tuple-element.100, f32[32,4096]{0,1:T(8,128)S(1)} %copy.69, f32[]{:T(128)} %constant.382.clone.1), kind=kCustom, calls=%fused_computation.13 | custom fusion | bytes 2621444 | tf_op jit(solution)/shard_map/scatter | solution.py:61
  369.9 8.5 all-to-all-start.1
  378.4 15.5 %scatter_custom_fusion.1 = s32[4096]{0:T(1024)S(1)} fusion(s32[4096]{0:T(1024)S(1)} %get-tuple-element.100, s32[4096]{0:T(1024)S(1)} %iota.176, s32[]{:T(128)} %copy.148), kind=kCustom, calls=%fused_computation.235 | custom fusion | bytes 16388 | tf_op jit(solution)/shard_map/scatter | solution.py:54
  404.1 44.0 %all-gather.7.cloned.1.call-done = f32[512,1024]{0,1:T(8,128)} async-done(((f32[512,64]{0,1:T(8,128)}), f32[512,1024]{0,1:T(8,128)}) %all-gather.7.cloned.1.call-update) | async-done | bytes 2097168 | tf_op jit(solution)/shard_map/all_gather | solution.py:108
  450.3 24.4 %all-gather.11.cloned.1.call-done = f32[1024,256]{1,0:T(8,128)} async-done(((f32[128,256]{1,0:T(8,128)}), f32[1024,256]{1,0:T(8,128)}) %all-gather.11.cloned.1.call-update) | async-done | bytes 1048592 | tf_op jit(solution)/shard_map/all_gather | solution.py:117
  481.7 27.4 %all-gather.9.cloned.1.call-done = f32[1024,1024]{1,0:T(8,128)} async-done(((f32[128,1024]{1,0:T(8,128)}), f32[1024,1024]{1,0:T(8,128)}) %all-gather.9.cloned.1.call-update) | async-done | bytes 4194320 | tf_op jit(solution)/shard_map/all_gather | solution.py:116
  513.8 5.5 copy.54
  525.7 11.7 %cholesky.223 = f32[128,128]{1,0:T(8,128)S(1)} custom-call(f32[128,128]{1,0:T(8,128)S(1)} %cholesky.580), custom_call_target="Cholesky" | custom-call | tf_op jit(solution)/shard_map/jit(cholesky)/cholesky | solution.py:127
  539.9 9.8 %custom-call.64 = f32[1,128,128]{1,2,0:T(8,128)S(1)} custom-call(f32[1,128,128]{2,1,0:T(8,128)S(1)} %get-tuple-element.98), custom_call_target="InvertDiagBlocksLowerTriangular" | custom-call | tf_op jit(solution)/shard_map/jit(cholesky)/cholesky | solution.py:127
  553.7 11.9 %cholesky.244 = f32[128,128]{1,0:T(8,128)S(1)} custom-call(f32[128,128]{1,0:T(8,128)S(1)} %cholesky.584), custom_call_target="Cholesky" | custom-call | tf_op jit(solution)/shard_map/jit(cholesky)/cholesky | solution.py:127
  567.5 9.8 %custom-call.65 = f32[1,128,128]{1,2,0:T(8,128)S(1)} custom-call(f32[1,128,128]{2,1,0:T(8,128)S(1)} %get-tuple-element.95), custom_call_target="InvertDiagBlocksLowerTriangular" | custom-call | tf_op jit(solution)/shard_map/jit(cholesky)/cholesky | solution.py:127
  580.7 11.7 %cholesky.468 = f32[128,128]{1,0:T(8,128)S(1)} custom-call(f32[128,128]{1,0:T(8,128)S(1)} %cholesky.589), custom_call_target="Cholesky" | custom-call | tf_op jit(solution)/shard_map/jit(cholesky)/cholesky | solution.py:127
  593.7 9.8 %custom-call.66 = f32[1,128,128]{1,2,0:T(8,128)S(1)} custom-call(f32[1,128,128]{2,1,0:T(8,128)S(1)} %get-tuple-element.92), custom_call_target="InvertDiagBlocksLowerTriangular" | custom-call | tf_op jit(solution)/shard_map/jit(cholesky)/cholesky | solution.py:127
  607.1 12.1 %cholesky.487 = f32[128,128]{1,0:T(8,128)S(1)} custom-call(f32[128,128]{1,0:T(8,128)S(1)} %cholesky.594), custom_call_target="Cholesky" | custom-call | tf_op jit(solution)/shard_map/jit(cholesky)/cholesky | solution.py:127
  620.5 9.8 %custom-call.67 = f32[1,128,128]{1,2,0:T(8,128)S(1)} custom-call(f32[1,128,128]{2,1,0:T(8,128)S(1)} %get-tuple-element.89), custom_call_target="InvertDiagBlocksLowerTriangular" | custom-call | tf_op jit(solution)/shard_map/jit(cholesky)/cholesky | solution.py:127
  633.8 11.7 %cholesky.506 = f32[128,128]{1,0:T(8,128)S(1)} custom-call(f32[128,128]{1,0:T(8,128)S(1)} %cholesky.599), custom_call_target="Cholesky" | custom-call | tf_op jit(solution)/shard_map/jit(cholesky)/cholesky | solution.py:127
  646.8 9.9 %custom-call.68 = f32[1,128,128]{1,2,0:T(8,128)S(1)} custom-call(f32[1,128,128]{2,1,0:T(8,128)S(1)} %get-tuple-element.86), custom_call_target="InvertDiagBlocksLowerTriangular" | custom-call | tf_op jit(solution)/shard_map/jit(cholesky)/cholesky | solution.py:127
  660.1 11.7 %cholesky.526 = f32[128,128]{1,0:T(8,128)S(1)} custom-call(f32[128,128]{1,0:T(8,128)S(1)} %cholesky.604), custom_call_target="Cholesky" | custom-call | tf_op jit(solution)/shard_map/jit(cholesky)/cholesky | solution.py:127
  673.1 9.8 %custom-call.69 = f32[1,128,128]{1,2,0:T(8,128)S(1)} custom-call(f32[1,128,128]{2,1,0:T(8,128)S(1)} %get-tuple-element.83), custom_call_target="InvertDiagBlocksLowerTriangular" | custom-call | tf_op jit(solution)/shard_map/jit(cholesky)/cholesky | solution.py:127
  685.9 11.9 %cholesky.546 = f32[128,128]{1,0:T(8,128)S(1)} custom-call(f32[128,128]{1,0:T(8,128)S(1)} %cholesky.609), custom_call_target="Cholesky" | custom-call | tf_op jit(solution)/shard_map/jit(cholesky)/cholesky | solution.py:127
  699.1 9.8 %custom-call.70 = f32[1,128,128]{1,2,0:T(8,128)S(1)} custom-call(f32[1,128,128]{2,1,0:T(8,128)S(1)} %get-tuple-element.80), custom_call_target="InvertDiagBlocksLowerTriangular" | custom-call | tf_op jit(solution)/shard_map/jit(cholesky)/cholesky | solution.py:127
  711.5 11.7 %cholesky.564 = f32[128,128]{1,0:T(8,128)S(1)} custom-call(f32[128,128]{1,0:T(8,128)S(1)} %convolution_subtract_fusion.21), custom_call_target="Cholesky" | custom-call | tf_op jit(solution)/shard_map/jit(cholesky)/cholesky | solution.py:127
  734.6 28.0 %while.1 = (s32[]{:T(128)}, f32[1024,1024]{1,0:T(8,128)}, s32[8,2]{0,1:T(2,128)S(1)}, f32[8,128,128]{2,1,0:T(8,128)}, s32[]{:T(128)}) while((s32[]{:T(128)}, f32[1024,1024]{1,0:T(8,128)}, s32[8,2]{0,1:T(2,128)S(1)}, f32[8,128,128]{2,1,0:T(8,128)}, s32[]{:T(128)}) %tuple.90), condition=%wide.while_cond, body=%wide.while_body.sunk | while | flops 2 | bytes 132705 | solution.py:128
  762.6 79.8 %custom-call.71 = f32[8,128,128]{1,2,0:T(8,128)S(1)} custom-call(f32[8,128,128]{2,1,0:T(8,128)} %get-tuple-element.9), custom_call_target="InvertDiagBlocksLowerTriangular" | custom-call | tf_op jit(solution)/shard_map/triangular_solve | solution.py:128
  (177 shorter events, 147.4 us)
Async XLA Ops:
  7.2 1.1 copy-start
  7.2 296.7 %all-gather.5.cloned.1.call-start = ((), (), s32[]{:S(2)}) async-start(), calls=%async_computation.2 | async-start | bytes 16908288 | tf_op jit(solution)/shard_map/all_gather | solution.py:65
  17.4 12.0 %copy-start.9 = (s32[4096]{0:T(1024)S(1)}, s32[4096]{0:T(1024)}, u32[]{:S(2)}) copy-start(s32[4096]{0:T(1024)} %param.8) | copy-start | bytes 49156
  17.4 12.2 %copy-start.10 = (f32[4]{0:T(128)S(1)}, f32[4]{0:T(128)}, u32[]{:S(2)}) copy-start(f32[4]{0:T(128)} %constant.397.clone) | copy-start | bytes 52
  17.4 272.3 %all-to-all-start = ((bf16[128,4,32,512]{3,2,1,0:T(8,128)(2,1)}), bf16[128,4,32,512]{3,2,1,0:T(8,128)(2,1)}, u32[]{:S(2)}, u32[]{:S(2)}) async-start(bf16[128,4,32,512]{3,2,1,0:T(8,128)(2,1)} %stack.3), calls=%async_computation | async-start | bytes 33554432 | tf_op jit(solution)/shard_map/all_to_all | solution.py:67
  30.0 273.8 %copy-start.4 = (bf16[128,512]{1,0:T(8,128)(2,1)S(1)}, bf16[128,512]{1,0:T(8,128)(2,1)}, u32[]{:S(2)}) copy-start(bf16[128,512]{1,0:T(8,128)(2,1)} %convolution_convert_fusion.1) | copy-start | bytes 393220
  369.9 31.1 %all-to-all-start.1 = ((f32[128,8,256]{2,1,0:T(8,128)}), f32[128,8,256]{2,1,0:T(8,128)S(1)}, u32[]{:S(2)}, u32[]{:S(2)}) async-start(f32[128,8,256]{2,1,0:T(8,128)} %reshape_reshape.7), calls=%async_computation.1 | async-start | bytes 2097152 | tf_op jit(solution)/shard_map/all_to_all | solution.py:90
  378.3 69.8 %all-gather.7.cloned.1.call-start = ((), (), s32[]{:S(2)}) async-start(), calls=%async_computation.3 | async-start | bytes 2228224 | tf_op jit(solution)/shard_map/all_gather | solution.py:108
  403.3 71.4 %all-gather.11.cloned.1.call-start = ((), (), s32[]{:S(2)}) async-start(), calls=%async_computation.5 | async-start | bytes 1179648 | tf_op jit(solution)/shard_map/all_gather | solution.py:117
  404.1 105.0 %all-gather.9.cloned.1.call-start = ((), (), s32[]{:S(2)}) async-start(), calls=%async_computation.4 | async-start | bytes 4718592 | tf_op jit(solution)/shard_map/all_gather | solution.py:116
  523.8 1.9 copy-start.3
  842.4 6.0 copy-start.2
  849.4 7.1 copy-start.5
  851.0 6.6 copy-start.6
  856.5 4.7 copy-start.8
  863.0 6.2 copy-start.7
  868.8 9.0 %copy-start.1 = (bf16[512,512]{1,0:T(8,128)(2,1)S(1)}, bf16[512,512]{1,0:T(8,128)(2,1)}, u32[]{:S(2)}) copy-start(bf16[512,512]{1,0:T(8,128)(2,1)} %param.6) | copy-start | bytes 1572868
Sparse Core Ops, SparseCore 0:
  11.6 248.3 all-gather.4
  403.4 44.6 all-gather.6
  449.9 24.7 all-gather.10
  476.8 32.1 all-gather.8
